TPU v7x, 32 devices: a whole 2x2x4 slice. The times are simulated.
32 devices in a mesh: group: 1, expert: 16 (over z, y, x), dp: 2 (over core).
Axes of the slice: x: 2, y: 2, z: 4, core: 2. Of those that a mesh axis runs over, the one named last changes fastest.
Arguments:
- tokens: bfloat16 [2048, 4096], P(('group', 'expert', 'dp')), may hold values from -6 to 6
- queries: bfloat16 [2048, 4096], P(('group', 'expert', 'dp')), may hold values from -6 to 6
- keys_local: bfloat16 [2048, 256], P(('group', 'expert', 'dp')), may hold values from -6 to 6
- values_local: bfloat16 [2048, 256], P(('group', 'expert', 'dp')), may hold values from -6 to 6
- prompt_keys: bfloat16 [1024, 256], P('group'), may hold values from -6 to 6
- prompt_values: bfloat16 [1024, 256], P('group'), may hold values from -6 to 6
- norm_gain: float32 [4096], replicated, may hold values from 0.25 to 1.75
- expert_ids: int32 [2048, 8], P(('group', 'expert', 'dp')), may hold values from 0 to 15, all different within a row; in each aligned block of 64 rows (0 to 63, 64 to 127, ...) at most 42 rows name the same one
- route_weight: float32 [2048, 8], P(('group', 'expert', 'dp')), may hold values from 0.05 to 1
- stored_gate: bfloat16 [16, 4096, 768], P('expert', None, 'dp'), may hold values from -0.09375 to 0.09375
- stored_up: bfloat16 [16, 4096, 768], P('expert', None, 'dp'), may hold values from -0.09375 to 0.09375
- stored_down: bfloat16 [16, 768, 4096], P('expert', 'dp'), may hold values from -0.21875 to 0.21875
- holder: int32 [16], replicated, may hold values from 0 to 15, as said below
Outputs:
- layer_out: bfloat16 [2048, 4096], P(('group', 'expert', 'dp'))
Inputs may be any that keep to these rules, and one draw needn't show every extreme that they name: `expert_ids`: each row names 8 different experts. In the 64 rows of one device no expert is named more than 42 times, and in every draw some expert is named exactly 42 times in some device's rows. holder[s] is s or the slot 8 away (s + 16 / 2 modulo 16), holder[holder[s]] = s, and holder[0] = 8.
All inputs are finite; a program needn't handle non-finite values.
Results may differ from a plain program's by a relative error of at most 0.0055.
Values may be sent and summed in bfloat16 or wider, within the bound.
No kernel may reach another device: no remote copies, remote signals or barrier semaphores. Data moves between devices by JAX's collectives and lax.ppermute only.
A program may use at most 192 MiB of HBM per device.

v0:
```python
import jax
import jax.numpy as jnp
from jax import lax
from jax.sharding import PartitionSpec as P

HEADS = 32
KVH = 2
HD = 128
TOPK = 8
EXP_DEV = 1
PREFIX = 1024


def attend_rows(queries, keys_local, values_local, prompt_keys, prompt_values):
    count_rows = queries.shape[0]
    grouping = HEADS // KVH
    query_all = queries.reshape(count_rows, KVH, grouping, HD)
    key_all = jnp.concatenate([prompt_keys, keys_local], 0).reshape(-1, KVH, HD)
    value_all = jnp.concatenate([prompt_values, values_local], 0).reshape(-1, KVH, HD)
    scores = jnp.einsum(
        "tkgd,skd->kgts", query_all, key_all, preferred_element_type=jnp.float32
    ) * HD ** (-0.5)
    column = jnp.arange(key_all.shape[0], dtype=jnp.int32)
    row_index = jnp.arange(count_rows, dtype=jnp.int32)
    allowed = (column[None, :] < PREFIX) | (column[None, :] - PREFIX <= row_index[:, None])
    scores = jnp.where(allowed[None, None], scores, -jnp.inf)
    highest = jnp.max(scores, axis=-1, keepdims=True)
    expons = jnp.exp(scores - highest)
    weights = (expons / jnp.sum(expons, axis=-1, keepdims=True)).astype(jnp.bfloat16)
    context = jnp.einsum("kgts,skd->tkgd", weights, value_all, preferred_element_type=jnp.float32)
    return context.reshape(count_rows, HEADS * HD)


def expert_rows(picked, gate_w, up_w, down_w):
    gate_val = jnp.dot(picked, gate_w, preferred_element_type=jnp.float32)
    up_val = jnp.dot(picked, up_w, preferred_element_type=jnp.float32)
    hidden = (jax.nn.silu(gate_val) * up_val).astype(jnp.bfloat16)
    return jnp.dot(hidden, down_w, preferred_element_type=jnp.float32).astype(jnp.bfloat16)


def local(
    tokens,
    queries,
    keys_local,
    values_local,
    prompt_keys,
    prompt_values,
    norm_gain,
    expert_ids,
    route_weight,
    stored_gate,
    stored_up,
    stored_down,
    holder,
):
    owners = lax.axis_size("expert")
    tok_count = tokens.shape[0]
    model_width = tokens.shape[1]
    capacity = min(tok_count, max(2, tok_count * TOPK * 4 // (3 * owners * EXP_DEV)))
    gate_w = stored_gate[0]
    up_w = stored_up[0]
    down_w = stored_down[0]
    context = attend_rows(queries, keys_local, values_local, prompt_keys, prompt_values)
    widened = tokens.astype(jnp.float32)
    normed = (
        widened * lax.rsqrt(jnp.mean(widened * widened, axis=-1, keepdims=True) + 1e-06) * norm_gain
    ).astype(jnp.bfloat16)
    shares = route_weight / jnp.sum(route_weight, axis=-1, keepdims=True)
    flat_ids = expert_ids.reshape(-1)
    onehot = (flat_ids[:, None] == jnp.arange(owners, dtype=jnp.int32)[None, :]).astype(jnp.int32)
    earlier = jnp.cumsum(onehot, axis=0) - onehot
    slot_of = jnp.sum(earlier * onehot, axis=1)
    places = (holder[flat_ids] * capacity + slot_of).reshape(tok_count, TOPK)
    chooser = (
        (jnp.arange(owners * capacity, dtype=jnp.int32)[:, None, None] == places[None])
        .any(axis=2)
        .astype(jnp.bfloat16)
    )
    send_rows = (
        jnp.dot(chooser, normed, preferred_element_type=jnp.float32)
        .astype(jnp.bfloat16)
        .reshape(owners, capacity, model_width)
    )
    both_rows = lax.all_gather(
        lax.all_to_all(send_rows, "expert", split_axis=0, concat_axis=0, tiled=True)[None],
        "dp",
        axis=0,
        tiled=True,
    )
    partial_out = expert_rows(both_rows.reshape(-1, model_width), gate_w, up_w, down_w)
    partial_out = partial_out.astype(jnp.float32).reshape(both_rows.shape)
    own_sum = lax.psum_scatter(
        partial_out.astype(jnp.bfloat16), "dp", scatter_dimension=0, tiled=True
    ).astype(jnp.float32)[0]
    results = lax.all_to_all(
        own_sum.astype(jnp.bfloat16), "expert", split_axis=0, concat_axis=0, tiled=True
    )
    gathered = results.reshape(owners * capacity, model_width)[places]
    mixture = jnp.einsum("tk,tkd->td", shares, gathered.astype(jnp.float32))
    return (widened + context + mixture).astype(jnp.bfloat16)


def solution(mesh):
    return jax.shard_map(
        local,
        mesh=mesh,
        in_specs=(
            P(("group", "expert", "dp"), None),
            P(("group", "expert", "dp"), None),
            P(("group", "expert", "dp"), None),
            P(("group", "expert", "dp"), None),
            P("group", None),
            P("group", None),
            P(),
            P(("group", "expert", "dp"), None),
            P(("group", "expert", "dp"), None),
            P("expert", None, "dp"),
            P("expert", None, "dp"),
            P("expert", "dp", None),
            P(),
        ),
        out_specs=P(("group", "expert", "dp"), None),
        check_vma=False,
    )
```

profile of v0, /device:TPU:14, one launch (start us, length us, event | category | flops | bytes accessed | tf_op | source)
XLA Modules:
  0.0 474.5 jit_solution(1100816948195221598)
XLA Ops:
  7.7 2.0 fusion.56
  9.7 4.4 compare_select_fusion.2
  15.7 5.6 %fusion.48 = s32[512]{0:T(512)S(1)} fusion(s32[512]{0:T(512)S(1)} %fusion.46, pred[512]{0:T(512)(128)(4,1)S(1)} %get-tuple-element.13, pred[512]{0:T(512)(128)(4,1)S(1)} %get-tuple-element.12, pred[512]{0:T(512)(128)(4,1)S(1)} %get-tuple-element.11, pred[512]{0:T(512)(128)(4,1)S(1)} %get-tuple-element.10, pred[512]{0:T(512)(128)(4,1)S(1)} %get-tuple-element.9, ...), kind=kLoop, calls=%fused_computation.76 | loop fusion | flops 5632 | bytes 10788 | tf_op jit(solution)/shard_map/add | solution.py:73
  21.9 1.2 fusion.26
  23.2 5.2 %convolution_convert_fusion.1 = bf16[672,4096]{1,0:T(8,128)(2,1)} fusion(pred[672,64]{0,1:T(8,128)(4,1)S(1)} %fusion.20, bf16[64,4096]{1,0:T(8,128)(2,1)} %param.13, f32[4096]{0:T(1024)} %param.19, f32[64]{0:T(128)S(1)} %add_rsqrt_fusion), kind=kOutput, calls=%fused_computation.7 | convolution fusion | flops 356122624 | bytes 6088960 | tf_op jit(solution)/shard_map/dot_general | solution.py:80
  28.3 6.2 %reshape.183 = bf16[16,42,4096]{2,1,0:T(8,128)(2,1)} reshape(bf16[672,4096]{1,0:T(8,128)(2,1)} %convolution_convert_fusion.1) | data formatting | bytes 11010048 | tf_op jit(solution)/shard_map/reshape | solution.py:82
  34.5 143.7 %all_to_all.10 = bf16[16,42,4096]{2,1,0:T(8,128)(2,1)S(1)} all-to-all(bf16[16,42,4096]{2,1,0:T(8,128)(2,1)} %reshape.183), channel_id=1, replica_groups=mesh['group'=1,'expert'=16,'dp'=2] {'expert'}, dimensions={0} | all-to-all | bytes 11010048 | tf_op jit(solution)/shard_map/all_to_all | solution.py:85
  178.3 5.4 %copy.47 = bf16[16,42,4096]{2,0,1:T(8,128)(2,1)} copy(bf16[16,42,4096]{2,1,0:T(8,128)(2,1)S(1)} %all_to_all.10) | data formatting | bytes 11010048 | tf_op jit(solution)/shard_map/all_to_all | solution.py:85
  183.9 23.3 %all-gather.3.cloned.1.call-done = bf16[32,42,4096]{2,0,1:T(8,128)(2,1)} async-done(((bf16[16,42,4096]{2,0,1:T(8,128)(2,1)}), bf16[32,42,4096]{2,0,1:T(8,128)(2,1)}) %all-gather.3.cloned.1.call-update) | async-done | bytes 11010064 | tf_op jit(solution)/shard_map/all_gather | solution.py:84
  207.3 14.0 %copy.48 = bf16[32,42,4096]{2,1,0:T(8,128)(2,1)} copy(bf16[32,42,4096]{2,0,1:T(8,128)(2,1)} %all-gather.3.cloned.1.call-done) | data formatting | bytes 22020096 | tf_op jit(solution)/shard_map/all_gather | solution.py:84
  221.3 11.9 %reshape.184 = bf16[1344,4096]{1,0:T(8,128)(2,1)} reshape(bf16[32,42,4096]{2,1,0:T(8,128)(2,1)} %copy.48) | data formatting | bytes 22020096 | tf_op jit(solution)/shard_map/reshape | solution.py:90
  233.2 10.5 %fusion.10 = f32[1344,384]{1,0:T(8,128)} fusion(bf16[1344,4096]{1,0:T(8,128)(2,1)} %reshape.184, bf16[1,4096,384]{2,1,0:T(8,128)(2,1)} %param.22), kind=kOutput, calls=%fused_computation.17 | convolution fusion | flops 4227858432 | bytes 16220160 | tf_op jit(solution)/shard_map/dot_general | solution.py:35
  243.7 17.9 %convolution_convert_fusion = bf16[1344,4096]{1,0:T(8,128)(2,1)} fusion(bf16[1,384,4096]{2,1,0:T(8,128)(2,1)S(1)} %copy-done, bf16[1344,4096]{1,0:T(8,128)(2,1)} %reshape.184, bf16[1,4096,384]{2,1,0:T(8,128)(2,1)} %param.23, f32[1344,384]{1,0:T(8,128)} %fusion.10), kind=kOutput, calls=%fused_computation.2 | convolution fusion | flops 8464318464 | bytes 30375936 | tf_op jit(solution)/shard_map/dot_general | solution.py:38
  261.6 11.7 %convert_element_type.48 = bf16[2,16,42,4096]{3,2,1,0:T(8,128)(2,1)} reshape(bf16[1344,4096]{1,0:T(8,128)(2,1)} %convolution_convert_fusion) | data formatting | bytes 22020096 | tf_op jit(solution)/shard_map/convert_element_type | solution.py:93
  273.4 23.3 %reduce-scatter.2.cloned.1.call-done = bf16[1,16,42,4096]{3,2,1,0:T(8,128)(2,1)} async-done(((bf16[2,16,42,4096]{3,2,1,0:T(8,128)(2,1)}), bf16[1,16,42,4096]{3,2,1,0:T(8,128)(2,1)}) %reduce-scatter.2.cloned.1.call-update) | async-done | bytes 5505040 | tf_op jit(solution)/shard_map/reduce_scatter | solution.py:92
  296.7 7.1 %all-to-all-start.1 = ((bf16[16,42,4096]{2,1,0:T(8,128)(2,1)}), bf16[16,42,4096]{2,1,0:T(8,128)(2,1)}, u32[]{:S(2)}, u32[]{:S(2)}) async-start(bf16[16,42,4096]{2,1,0:T(8,128)(2,1)} %bitcast.96), calls=%async_computation.2 | async-start | bytes 12582912 | tf_op jit(solution)/shard_map/all_to_all | solution.py:95
  305.8 4.3 fusion.57
  310.1 5.9 %fusion.21 = f32[64,2,16,128]{3,0,2,1:T(8,128)S(1)} fusion(bf16[1088,2,128,1]{0,2,3,1:T(8,128)(2,1)S(1)} %bitcast.100, f32[2,16,64]{2,1,0:T(8,128)S(1)} %fusion.57, pred[64,1088]{1,0:T(8,128)(4,1)S(1)} %fusion.39, bf16[1088,2,128,1]{0,2,3,1:T(8,128)(2,1)S(1)} %bitcast.99, bf16[64,2,16,128]{3,2,1,0:T(8,128)(2,1)} %bitcast.103), kind=kOutput, calls=%fused_computation.28 | convolution fusion | flops 1151994880 | bytes 2764800 | tf_op jit(solution)/shard_map/kgts,skd->tkgd/dot_general | solution.py:30
  316.0 1.6 copy.42
  317.6 126.1 %all-to-all-done.1 = bf16[16,42,4096]{2,1,0:T(8,128)(2,1)} async-done(((bf16[16,42,4096]{2,1,0:T(8,128)(2,1)}), bf16[16,42,4096]{2,1,0:T(8,128)(2,1)}, u32[]{:S(2)}, u32[]{:S(2)}) %all-to-all-start.1) | async-done | bytes 5505056 | tf_op jit(solution)/shard_map/all_to_all | solution.py:95
  443.7 6.2 %reshape.185 = bf16[672,4096]{1,0:T(8,128)(2,1)} reshape(bf16[16,42,4096]{2,1,0:T(8,128)(2,1)} %all-to-all-done.1) | data formatting | bytes 11010048 | tf_op jit(solution)/shard_map/reshape | solution.py:98
  449.9 12.2 %gather_fusion = bf16[512,4096]{1,0:T(8,128)(2,1)} fusion(bf16[672,4096]{1,0:T(8,128)(2,1)} %reshape.185, s32[1024]{0:T(1024)S(1)} %pad_clamp_fusion), kind=kCustom, calls=%fused_computation | custom fusion | bytes 8390656 | tf_op jit(solution)/shard_map/gather | solution.py:98
  462.1 3.5 fusion.6
  465.7 1.9 fusion.25
  (53 shorter events, 5.6 us)
Async XLA Ops:
  6.5 237.2 %copy-start = (bf16[1,384,4096]{2,1,0:T(8,128)(2,1)S(1)}, bf16[1,384,4096]{2,1,0:T(8,128)(2,1)}, u32[]{:S(2)}) copy-start(bf16[1,384,4096]{2,1,0:T(8,128)(2,1)} %param.24) | copy-start | bytes 9437188
  6.5 200.7 %all-gather.3.cloned.1.call-start = ((), (), s32[]{:S(2)}) async-start(), calls=%async_computation.4 | async-start | bytes 16515072 | tf_op jit(solution)/shard_map/all_gather | solution.py:84
  183.7 112.9 %reduce-scatter.2.cloned.1.call-start = ((), (), s32[]{:S(2)}) async-start(), calls=%async_computation.3 | async-start | bytes 18874368 | tf_op jit(solution)/shard_map/reduce_scatter | solution.py:92
  296.6 7.3 %copy-start.9 = (f32[64,8]{0,1:T(8,128)S(1)}, f32[64,8]{0,1:T(8,128)}, u32[]{:S(2)}) copy-start(f32[64,8]{0,1:T(8,128)} %param.21) | copy-start | bytes 6148
  296.6 7.5 %copy-start.4 = (bf16[1024,256]{1,0:T(8,128)(2,1)S(1)}, bf16[1024,256]{1,0:T(8,128)(2,1)}, u32[]{:S(2)}) copy-start(bf16[1024,256]{1,0:T(8,128)(2,1)} %param.17) | copy-start | bytes 1572868
  296.6 7.5 %copy-start.7 = (bf16[64,256]{1,0:T(8,128)(2,1)S(1)}, bf16[64,256]{1,0:T(8,128)(2,1)}, u32[]{:S(2)}) copy-start(bf16[64,256]{1,0:T(8,128)(2,1)} %param.15) | copy-start | bytes 98308
  296.6 7.8 %copy-start.5 = (bf16[64,4096]{1,0:T(8,128)(2,1)S(1)}, bf16[64,4096]{1,0:T(8,128)(2,1)}, u32[]{:S(2)}) copy-start(bf16[64,4096]{1,0:T(8,128)(2,1)} %param.14) | copy-start | bytes 1572868
  296.6 8.7 %copy-start.6 = (bf16[1024,256]{1,0:T(8,128)(2,1)S(1)}, bf16[1024,256]{1,0:T(8,128)(2,1)}, u32[]{:S(2)}) copy-start(bf16[1024,256]{1,0:T(8,128)(2,1)} %param.18) | copy-start | bytes 1572868
  296.7 8.7 %copy-start.8 = (bf16[64,256]{1,0:T(8,128)(2,1)S(1)}, bf16[64,256]{1,0:T(8,128)(2,1)}, u32[]{:S(2)}) copy-start(bf16[64,256]{1,0:T(8,128)(2,1)} %param.16) | copy-start | bytes 98308
  296.7 147.0 %all-to-all-start.1 = ((bf16[16,42,4096]{2,1,0:T(8,128)(2,1)}), bf16[16,42,4096]{2,1,0:T(8,128)(2,1)}, u32[]{:S(2)}, u32[]{:S(2)}) async-start(bf16[16,42,4096]{2,1,0:T(8,128)(2,1)} %bitcast.96), calls=%async_computation.2 | async-start | bytes 12582912 | tf_op jit(solution)/shard_map/all_to_all | solution.py:95
  449.9 17.8 %copy-start.1 = (bf16[1,384,4096]{2,1,0:T(8,128)(2,1)S(1)}, bf16[1,384,4096]{2,1,0:T(8,128)(2,1)}, u32[]{:S(2)}) copy-start(bf16[1,384,4096]{2,1,0:T(8,128)(2,1)} %param.24) | copy-start | bytes 9437188
  462.1 3.6 copy-start.2
  462.1 3.6 copy-start.3
Sparse Core Ops, SparseCore 0:
  183.8 23.3 all-gather.2
  273.5 23.1 reduce-scatter.1
where the time goes:
time: 476 us; the launch traced here: 474 us
  waiting for transfers between devices  173 us (36%)
  blocking collectives  144 us (30%)
  local copies, waits for them, and re-layouts  74.5 us (16%)
  matrix products  47.4 us (10%)
  other arithmetic  15.2 us (3%)
  between operations  13.6 us (3%)
  starting transfers between devices  7.33 us (2%)
    all_to_all x1, blocking collectives, local(): lax.all_to_all(send_rows, 'expert', split_axis=0, concat_axis=0, tiled=True)  144 us
    all_to_all x1, waiting for transfers between devices, local(): lax.all_to_all(own_sum.astype(jnp.bfloat16), 'expert', split_axis=0, conc...  126 us
    all_gather x1, waiting for transfers between devices, local(): lax.all_gather(lax.all_to_all(send_rows, 'expert', split_axis=0, concat_a...  23.3 us
    reduce_scatter x1, waiting for transfers between devices, local(): lax.psum_scatter(partial_out.astype(jnp.bfloat16), 'dp', scatter_dimensio...  23.3 us
    dot_general x1, matrix products, expert_rows(): jnp.dot(hidden, down_w, preferred_element_type=jnp.float32)  17.9 us
    all_gather x1, local copies, waits for them, and re-layouts, local(): lax.all_gather(lax.all_to_all(send_rows, 'expert', split_axis=0, concat_a...  14 us
    gather x1, local copies, waits for them, and re-layouts, local(): gathered = results.reshape(owners * capacity, model_width)[places]  12.2 us
    reshape x1, local copies, waits for them, and re-layouts, local(): both_rows.reshape(-1, model_width)  11.9 us
  transfers between devices with their start and end apart: 3, of which 3 were waited for; matrix products, arithmetic and copies ran while one was open for 3% of the time, Pallas kernels for 0%

commit v1 on v0

--- a/solution.py
+++ b/solution.py
@@ -9,6 +9,26 @@
 TOPK = 8
 EXP_DEV = 1
 PREFIX = 1024
+
+
+def _try_all_bars(xs, group_axis):
+    then = jax.lax.axis_size(group_axis)
+    next_value = jax.lax.axis_index(group_axis)
+    state_next, plain = (then, next_value)
+    far_arr = xs.shape[0] // state_next
+    arr_out = jnp.roll(xs, shift=-plain * far_arr, axis=0)
+    p_next = lax.slice_in_dim(arr_out, 0, far_arr, axis=0)
+    log = [p_next]
+    for q in tuple(range(1, state_next)):
+        all_values = lax.slice_in_dim(arr_out, q * far_arr, (q + 1) * far_arr, axis=0)
+        log.append(
+            jax.lax.ppermute(
+                all_values, group_axis, [(ii, (ii + q) % state_next) for ii in range(state_next)]
+            )
+        )
+    value_now = jnp.concatenate(log[::-1], 0)
+    r_now = jnp.roll(value_now, (plain + 1) * log[0].shape[0], 0)
+    return r_now
 
 
 def attend_rows(queries, keys_local, values_local, prompt_keys, prompt_values):
@@ -81,12 +101,7 @@
         .astype(jnp.bfloat16)
         .reshape(owners, capacity, model_width)
     )
-    both_rows = lax.all_gather(
-        lax.all_to_all(send_rows, "expert", split_axis=0, concat_axis=0, tiled=True)[None],
-        "dp",
-        axis=0,
-        tiled=True,
-    )
+    both_rows = lax.all_gather(_try_all_bars(send_rows, "expert")[None], "dp", axis=0, tiled=True)
     partial_out = expert_rows(both_rows.reshape(-1, model_width), gate_w, up_w, down_w)
     partial_out = partial_out.astype(jnp.float32).reshape(both_rows.shape)
     own_sum = lax.psum_scatter(

time: 476 us -> 536 us (1.13); the launches traced: 474 us -> 526 us
  blocking collectives: 144 us -> 0 us
  starting transfers between devices: 7.33 us -> 117 us
  waiting for transfers between devices: 173 us -> 237 us
  local copies, waits for them, and re-layouts: 74.5 us -> 85.9 us
  other arithmetic: 15.2 us -> 24.9 us
    all_to_all x1 -> x0, blocking collectives: 144 us -> none  [local(): lax.all_to_all(send_rows, 'expert', split_axis=0, concat_axis=0, tiled=True)]
    ppermute x0 -> x15, starting transfers between devices: none -> 109 us  [_try_all_bars(): jax.lax.ppermute(all_values, group_axis, [(ii, (ii + q) % state_next) for...]
    ppermute x0 -> x15, waiting for transfers between devices: none -> 54.8 us  [_try_all_bars(): jax.lax.ppermute(all_values, group_axis, [(ii, (ii + q) % state_next) for...]
    all_gather x1, waiting for transfers between devices: 23.3 us -> 32.8 us  [local(): lax.all_gather(_try_all_bars(send_rows, 'expert')[None], 'dp', axis=0, ti...]
    concatenate x0 -> x2, other arithmetic: none -> 8.3 us  [the longest x1 5.15 us: _try_all_bars(): arr_out = jnp.roll(xs, shift=-plain * far_arr, axis=0)]
    unnamed x22 -> x37, local copies, waits for them, and re-layouts: 1.86 us -> 9.88 us
    dynamic_slice x0 -> x1, local copies, waits for them, and re-layouts: none -> 5.4 us  [_try_all_bars(): r_now = jnp.roll(value_now, (plain + 1) * log[0].shape[0], 0)]
    all_to_all x1 -> x0, local copies, waits for them, and re-layouts: 5.4 us -> none  [local(): lax.all_to_all(send_rows, 'expert', split_axis=0, concat_axis=0, tiled=True)]
  transfers between devices with their start and end apart: 3 -> 18, of which waited for: 3 -> 9; matrix products, arithmetic and copies ran while one was open for 3% -> 4% of each run, Pallas kernels for 0% -> 0%
where the time goes in v1:
time: 536 us; the launch traced here: 526 us
  waiting for transfers between devices  237 us (44%)
  starting transfers between devices  117 us (22%)
  local copies, waits for them, and re-layouts  85.9 us (16%)
  matrix products  47.3 us (9%)
  other arithmetic  24.9 us (5%)
  between operations  14 us (3%)
    all_to_all x1, waiting for transfers between devices, local(): lax.all_to_all(own_sum.astype(jnp.bfloat16), 'expert', split_axis=0, conc...  126 us
    ppermute x15, starting transfers between devices, _try_all_bars(): jax.lax.ppermute(all_values, group_axis, [(ii, (ii + q) % state_next) for...  109 us
    ppermute x15, waiting for transfers between devices, _try_all_bars(): jax.lax.ppermute(all_values, group_axis, [(ii, (ii + q) % state_next) for...  54.8 us
    all_gather x1, waiting for transfers between devices, local(): lax.all_gather(_try_all_bars(send_rows, 'expert')[None], 'dp', axis=0, ti...  32.8 us
    reduce_scatter x1, waiting for transfers between devices, local(): lax.psum_scatter(partial_out.astype(jnp.bfloat16), 'dp', scatter_dimensio...  23.3 us
    dot_general x1, matrix products, expert_rows(): jnp.dot(hidden, down_w, preferred_element_type=jnp.float32)  17.9 us
    all_gather x1, local copies, waits for them, and re-layouts, local(): lax.all_gather(_try_all_bars(send_rows, 'expert')[None], 'dp', axis=0, ti...  14 us
    gather x1, local copies, waits for them, and re-layouts, local(): gathered = results.reshape(owners * capacity, model_width)[places]  12.2 us
  transfers between devices with their start and end apart: 18, of which 9 were waited for; matrix products, arithmetic and copies ran while one was open for 4% of the time, Pallas kernels for 0%

profile of v1, /device:TPU:14, one launch (start us, length us, event | category | flops | bytes accessed | tf_op | source)
XLA Modules:
  0.0 526.2 jit_solution(696704912942831334)
XLA Ops:
  15.7 5.6 %fusion.50 = s32[512]{0:T(512)S(1)} fusion(s32[512]{0:T(512)S(1)} %fusion.48, pred[512]{0:T(512)(128)(4,1)S(1)} %get-tuple-element.14, pred[512]{0:T(512)(128)(4,1)S(1)} %get-tuple-element.13, pred[512]{0:T(512)(128)(4,1)S(1)} %get-tuple-element.12, pred[512]{0:T(512)(128)(4,1)S(1)} %get-tuple-element.11, pred[512]{0:T(512)(128)(4,1)S(1)} %get-tuple-element.10, ...), kind=kLoop, calls=%fused_computation.98 | loop fusion | flops 5632 | bytes 10788 | tf_op jit(solution)/shard_map/add | solution.py:93
  23.2 5.2 convolution_convert_fusion.1
  28.4 6.2 %reshape.183 = bf16[16,42,4096]{2,1,0:T(8,128)(2,1)} reshape(bf16[672,4096]{1,0:T(8,128)(2,1)} %convolution_convert_fusion.1) | data formatting | bytes 11010048 | tf_op jit(solution)/shard_map/reshape | solution.py:102
  51.9 12.9 %collective-permute-done = bf16[1,42,4096]{2,1,0:T(8,128)(2,1)} collective-permute-done((bf16[1,42,4096]{2,1,0:T(8,128)(2,1)}, bf16[1,42,4096]{2,1,0:T(8,128)(2,1)}, u32[]{:S(2)}, u32[]{:S(2)}) %collective-permute-start) | collective-permute-done | bytes 344096 | tf_op jit(solution)/shard_map/ppermute | solution.py:25
  66.8 12.1 %collective-permute-start.6 = (bf16[1,42,4096]{2,1,0:T(8,128)(2,1)}, bf16[1,42,4096]{2,1,0:T(8,128)(2,1)S(1)}, u32[]{:S(2)}, u32[]{:S(2)}) collective-permute-start(bf16[1,42,4096]{2,1,0:T(8,128)(2,1)} %get-tuple-element.25), channel_id=1, source_target_pairs={{0,18},{2,20},{4,22},{6,24},{8,26},{10,28},{12,30},{14,0},{16,2},{... | collective-permute-start | bytes 1032200 | tf_op jit(solution)/shard_map/ppermute | solution.py:25
  86.4 22.2 %collective-permute-done.4 = bf16[1,42,4096]{2,1,0:T(8,128)(2,1)} collective-permute-done((bf16[1,42,4096]{2,1,0:T(8,128)(2,1)}, bf16[1,42,4096]{2,1,0:T(8,128)(2,1)}, u32[]{:S(2)}, u32[]{:S(2)}) %collective-permute-start.4) | collective-permute-done | bytes 344096 | tf_op jit(solution)/shard_map/ppermute | solution.py:25
  109.6 9.9 %collective-permute-start.10 = (bf16[1,42,4096]{2,1,0:T(8,128)(2,1)}, bf16[1,42,4096]{2,1,0:T(8,128)(2,1)S(1)}, u32[]{:S(2)}, u32[]{:S(2)}) collective-permute-start(bf16[1,42,4096]{2,1,0:T(8,128)(2,1)} %get-tuple-element.21), channel_id=1, source_target_pairs={{0,10},{2,12},{4,14},{6,16},{8,18},{10,20},{12,22},{14,24},{16,26}... | collective-permute-start | bytes 1032200 | tf_op jit(solution)/shard_map/ppermute | solution.py:25
  127.1 28.2 %collective-permute-start.12 = (bf16[1,42,4096]{2,1,0:T(8,128)(2,1)}, bf16[1,42,4096]{2,1,0:T(8,128)(2,1)S(1)}, u32[]{:S(2)}, u32[]{:S(2)}) collective-permute-start(bf16[1,42,4096]{2,1,0:T(8,128)(2,1)} %get-tuple-element.19), channel_id=1, source_target_pairs={{0,6},{2,8},{4,10},{6,12},{8,14},{10,16},{12,18},{14,20},{16,22},{... | collective-permute-start | bytes 1032200 | tf_op jit(solution)/shard_map/ppermute | solution.py:25
  155.3 33.0 %collective-permute-start.13 = (bf16[1,42,4096]{2,1,0:T(8,128)(2,1)S(1)}, bf16[1,42,4096]{2,1,0:T(8,128)(2,1)S(1)}, u32[]{:S(2)}, u32[]{:S(2)}) collective-permute-start(bf16[1,42,4096]{2,1,0:T(8,128)(2,1)S(1)} %copy-done.6), channel_id=1, source_target_pairs={{0,4},{2,6},{4,8},{6,10},{8,12},{10,14},{12,16},{14,18},{16,20},{1... | collective-permute-start | bytes 1032200 | tf_op jit(solution)/shard_map/ppermute | solution.py:25
  188.4 9.9 %collective-permute-start.14 = (bf16[1,42,4096]{2,1,0:T(8,128)(2,1)S(1)}, bf16[1,42,4096]{2,1,0:T(8,128)(2,1)S(1)}, u32[]{:S(2)}, u32[]{:S(2)}) collective-permute-start(bf16[1,42,4096]{2,1,0:T(8,128)(2,1)S(1)} %get-tuple-element.17), channel_id=1, source_target_pairs={{0,2},{2,4},{4,6},{6,8},{8,10},{10,12},{12,14},{14,16},{16,18},{18... | collective-permute-start | bytes 1032200 | tf_op jit(solution)/shard_map/ppermute | solution.py:25
  206.9 7.6 %collective-permute-done.14 = bf16[1,42,4096]{2,1,0:T(8,128)(2,1)S(1)} collective-permute-done((bf16[1,42,4096]{2,1,0:T(8,128)(2,1)S(1)}, bf16[1,42,4096]{2,1,0:T(8,128)(2,1)S(1)}, u32[]{:S(2)}, u32[]{:S(2)}) %collective-permute-start.14) | collective-permute-done | bytes 344096 | tf_op jit(solution)/shard_map/ppermute | solution.py:25
  218.8 5.4 %copy.47 = bf16[16,42,4096]{2,0,1:T(8,128)(2,1)} copy(bf16[16,42,4096]{2,1,0:T(8,128)(2,1)S(1)} %fusion.2) | data formatting | bytes 11010048 | tf_op jit(solution)/shard_map/jit(_roll_dynamic)/dynamic_slice | solution.py:30
  224.7 32.8 %all-gather.3.cloned.1.call-done = bf16[32,42,4096]{2,0,1:T(8,128)(2,1)} async-done(((bf16[16,42,4096]{2,0,1:T(8,128)(2,1)}), bf16[32,42,4096]{2,0,1:T(8,128)(2,1)}) %all-gather.3.cloned.1.call-update) | async-done | bytes 11010064 | tf_op jit(solution)/shard_map/all_gather | solution.py:104
  257.5 14.0 %copy.48 = bf16[32,42,4096]{2,1,0:T(8,128)(2,1)} copy(bf16[32,42,4096]{2,0,1:T(8,128)(2,1)} %all-gather.3.cloned.1.call-done) | data formatting | bytes 22020096 | tf_op jit(solution)/shard_map/all_gather | solution.py:104
  271.6 11.9 %reshape.184 = bf16[1344,4096]{1,0:T(8,128)(2,1)} reshape(bf16[32,42,4096]{2,1,0:T(8,128)(2,1)} %copy.48) | data formatting | bytes 22020096 | tf_op jit(solution)/shard_map/reshape | solution.py:105
  283.4 10.6 %fusion.12 = f32[1344,384]{1,0:T(8,128)} fusion(bf16[1344,4096]{1,0:T(8,128)(2,1)} %reshape.184, bf16[1,4096,384]{2,1,0:T(8,128)(2,1)} %param.24), kind=kOutput, calls=%fused_computation.23 | convolution fusion | flops 4227858432 | bytes 16220160 | tf_op jit(solution)/shard_map/dot_general | solution.py:55
  294.0 17.9 %convolution_convert_fusion = bf16[1344,4096]{1,0:T(8,128)(2,1)} fusion(bf16[1,384,4096]{2,1,0:T(8,128)(2,1)S(1)} %copy-done, bf16[1344,4096]{1,0:T(8,128)(2,1)} %reshape.184, bf16[1,4096,384]{2,1,0:T(8,128)(2,1)} %param.25, f32[1344,384]{1,0:T(8,128)} %fusion.12), kind=kOutput, calls=%fused_computation.2 | convolution fusion | flops 8464318464 | bytes 30375936 | tf_op jit(solution)/shard_map/dot_general | solution.py:58
  311.9 11.7 %convert_element_type.48 = bf16[2,16,42,4096]{3,2,1,0:T(8,128)(2,1)} reshape(bf16[1344,4096]{1,0:T(8,128)(2,1)} %convolution_convert_fusion) | data formatting | bytes 22020096 | tf_op jit(solution)/shard_map/convert_element_type | solution.py:108
  323.6 23.3 %reduce-scatter.2.cloned.1.call-done = bf16[1,16,42,4096]{3,2,1,0:T(8,128)(2,1)} async-done(((bf16[2,16,42,4096]{3,2,1,0:T(8,128)(2,1)}), bf16[1,16,42,4096]{3,2,1,0:T(8,128)(2,1)}) %reduce-scatter.2.cloned.1.call-update) | async-done | bytes 5505040 | tf_op jit(solution)/shard_map/reduce_scatter | solution.py:107
  346.9 7.4 %all-to-all-start = ((bf16[16,42,4096]{2,1,0:T(8,128)(2,1)}), bf16[16,42,4096]{2,1,0:T(8,128)(2,1)}, u32[]{:S(2)}, u32[]{:S(2)}) async-start(bf16[16,42,4096]{2,1,0:T(8,128)(2,1)} %bitcast.96), calls=%async_computation.1 | async-start | bytes 12582912 | tf_op jit(solution)/shard_map/all_to_all | solution.py:110
  360.7 5.9 %fusion.23 = f32[64,2,16,128]{3,0,2,1:T(8,128)S(1)} fusion(bf16[1088,2,128,1]{0,2,3,1:T(8,128)(2,1)S(1)} %bitcast.100, f32[2,16,64]{2,1,0:T(8,128)S(1)} %fusion.60, pred[64,1088]{1,0:T(8,128)(4,1)S(1)} %fusion.41, bf16[1088,2,128,1]{0,2,3,1:T(8,128)(2,1)S(1)} %bitcast.99, bf16[64,2,16,128]{3,2,1,0:T(8,128)(2,1)} %bitcast.103), kind=kOutput, calls=%fused_computation.34 | convolution fusion | flops 1151994880 | bytes 2764800 | tf_op jit(solution)/shard_map/kgts,skd->tkgd/dot_general | solution.py:50
  368.2 125.8 %all-to-all-done = bf16[16,42,4096]{2,1,0:T(8,128)(2,1)} async-done(((bf16[16,42,4096]{2,1,0:T(8,128)(2,1)}), bf16[16,42,4096]{2,1,0:T(8,128)(2,1)}, u32[]{:S(2)}, u32[]{:S(2)}) %all-to-all-start) | async-done | bytes 5505056 | tf_op jit(solution)/shard_map/all_to_all | solution.py:110
  494.0 6.2 %reshape.185 = bf16[672,4096]{1,0:T(8,128)(2,1)} reshape(bf16[16,42,4096]{2,1,0:T(8,128)(2,1)} %all-to-all-done) | data formatting | bytes 11010048 | tf_op jit(solution)/shard_map/reshape | solution.py:113
  500.2 12.2 %gather_fusion = bf16[512,4096]{1,0:T(8,128)(2,1)} fusion(bf16[672,4096]{1,0:T(8,128)(2,1)} %reshape.185, s32[1024]{0:T(1024)S(1)} %pad_clamp_fusion), kind=kCustom, calls=%fused_computation | custom fusion | bytes 8390656 | tf_op jit(solution)/shard_map/gather | solution.py:113
  (101 shorter events, 74.3 us)
Async XLA Ops:
  6.5 287.4 %copy-start = (bf16[1,384,4096]{2,1,0:T(8,128)(2,1)S(1)}, bf16[1,384,4096]{2,1,0:T(8,128)(2,1)}, u32[]{:S(2)}) copy-start(bf16[1,384,4096]{2,1,0:T(8,128)(2,1)} %param.26) | copy-start | bytes 9437188
  6.5 251.0 %all-gather.3.cloned.1.call-start = ((), (), s32[]{:S(2)}) async-start(), calls=%async_computation.3 | async-start | bytes 16515072 | tf_op jit(solution)/shard_map/all_gather | solution.py:104
  44.8 20.0 %collective-permute-start = (bf16[1,42,4096]{2,1,0:T(8,128)(2,1)}, bf16[1,42,4096]{2,1,0:T(8,128)(2,1)}, u32[]{:S(2)}, u32[]{:S(2)}) collective-permute-start(bf16[1,42,4096]{2,1,0:T(8,128)(2,1)} %get-tuple-element.31), channel_id=1, source_target_pairs={{0,30},{2,0},{4,2},{6,4},{8,6},{10,8},{12,10},{14,12},{16,14},{18,... | collective-permute-start | bytes 1032200 | tf_op jit(solution)/shard_map/ppermute | solution.py:25
  45.3 21.5 %collective-permute-start.1 = (bf16[1,42,4096]{2,1,0:T(8,128)(2,1)}, bf16[1,42,4096]{2,1,0:T(8,128)(2,1)}, u32[]{:S(2)}, u32[]{:S(2)}) collective-permute-start(bf16[1,42,4096]{2,1,0:T(8,128)(2,1)} %get-tuple-element.30), channel_id=1, source_target_pairs={{0,28},{2,30},{4,0},{6,2},{8,4},{10,6},{12,8},{14,10},{16,12},{18,... | collective-permute-start | bytes 1032200 | tf_op jit(solution)/shard_map/ppermute | solution.py:25
  45.8 34.1 %collective-permute-start.2 = (bf16[1,42,4096]{2,1,0:T(8,128)(2,1)}, bf16[1,42,4096]{2,1,0:T(8,128)(2,1)}, u32[]{:S(2)}, u32[]{:S(2)}) collective-permute-start(bf16[1,42,4096]{2,1,0:T(8,128)(2,1)} %get-tuple-element.29), channel_id=1, source_target_pairs={{0,26},{2,28},{4,30},{6,0},{8,2},{10,4},{12,6},{14,8},{16,10},{18,... | collective-permute-start | bytes 1032200 | tf_op jit(solution)/shard_map/ppermute | solution.py:25
  48.2 32.9 %collective-permute-start.3 = (bf16[1,42,4096]{2,1,0:T(8,128)(2,1)}, bf16[1,42,4096]{2,1,0:T(8,128)(2,1)}, u32[]{:S(2)}, u32[]{:S(2)}) collective-permute-start(bf16[1,42,4096]{2,1,0:T(8,128)(2,1)} %get-tuple-element.28), channel_id=1, source_target_pairs={{0,24},{2,26},{4,28},{6,30},{8,0},{10,2},{12,4},{14,6},{16,8},{18,... | collective-permute-start | bytes 1032200 | tf_op jit(solution)/shard_map/ppermute | solution.py:25
  51.8 56.7 %collective-permute-start.4 = (bf16[1,42,4096]{2,1,0:T(8,128)(2,1)}, bf16[1,42,4096]{2,1,0:T(8,128)(2,1)}, u32[]{:S(2)}, u32[]{:S(2)}) collective-permute-start(bf16[1,42,4096]{2,1,0:T(8,128)(2,1)} %get-tuple-element.27), channel_id=1, source_target_pairs={{0,22},{2,24},{4,26},{6,28},{8,30},{10,0},{12,2},{14,4},{16,6},{18... | collective-permute-start | bytes 1032200 | tf_op jit(solution)/shard_map/ppermute | solution.py:25
  51.9 103.5 %copy-start.6 = (bf16[1,42,4096]{2,1,0:T(8,128)(2,1)S(1)}, bf16[1,42,4096]{2,1,0:T(8,128)(2,1)}, u32[]{:S(2)}) copy-start(bf16[1,42,4096]{2,1,0:T(8,128)(2,1)} %get-tuple-element.18) | copy-start | bytes 1032196
  64.8 44.8 %collective-permute-start.5 = (bf16[1,42,4096]{2,1,0:T(8,128)(2,1)}, bf16[1,42,4096]{2,1,0:T(8,128)(2,1)S(1)}, u32[]{:S(2)}, u32[]{:S(2)}) collective-permute-start(bf16[1,42,4096]{2,1,0:T(8,128)(2,1)} %get-tuple-element.26), channel_id=1, source_target_pairs={{0,20},{2,22},{4,24},{6,26},{8,28},{10,30},{12,0},{14,2},{16,4},{1... | collective-permute-start | bytes 1032200 | tf_op jit(solution)/shard_map/ppermute | solution.py:25
  66.8 52.7 %collective-permute-start.6 = (bf16[1,42,4096]{2,1,0:T(8,128)(2,1)}, bf16[1,42,4096]{2,1,0:T(8,128)(2,1)S(1)}, u32[]{:S(2)}, u32[]{:S(2)}) collective-permute-start(bf16[1,42,4096]{2,1,0:T(8,128)(2,1)} %get-tuple-element.25), channel_id=1, source_target_pairs={{0,18},{2,20},{4,22},{6,24},{8,26},{10,28},{12,30},{14,0},{16,2},{... | collective-permute-start | bytes 1032200 | tf_op jit(solution)/shard_map/ppermute | solution.py:25
  79.9 47.1 %collective-permute-start.7 = (bf16[1,42,4096]{2,1,0:T(8,128)(2,1)}, bf16[1,42,4096]{2,1,0:T(8,128)(2,1)S(1)}, u32[]{:S(2)}, u32[]{:S(2)}) collective-permute-start(bf16[1,42,4096]{2,1,0:T(8,128)(2,1)} %get-tuple-element.24), channel_id=1, source_target_pairs={{0,16},{2,18},{4,20},{6,22},{8,24},{10,26},{12,28},{14,30},{16,0},... | collective-permute-start | bytes 1032200 | tf_op jit(solution)/shard_map/ppermute | solution.py:25
  81.0 74.3 %collective-permute-start.8 = (bf16[1,42,4096]{2,1,0:T(8,128)(2,1)}, bf16[1,42,4096]{2,1,0:T(8,128)(2,1)S(1)}, u32[]{:S(2)}, u32[]{:S(2)}) collective-permute-start(bf16[1,42,4096]{2,1,0:T(8,128)(2,1)} %get-tuple-element.23), channel_id=1, source_target_pairs={{0,14},{2,16},{4,18},{6,20},{8,22},{10,24},{12,26},{14,28},{16,30}... | collective-permute-start | bytes 1032200 | tf_op jit(solution)/shard_map/ppermute | solution.py:25
  108.6 79.8 %collective-permute-start.9 = (bf16[1,42,4096]{2,1,0:T(8,128)(2,1)}, bf16[1,42,4096]{2,1,0:T(8,128)(2,1)S(1)}, u32[]{:S(2)}, u32[]{:S(2)}) collective-permute-start(bf16[1,42,4096]{2,1,0:T(8,128)(2,1)} %get-tuple-element.22), channel_id=1, source_target_pairs={{0,12},{2,14},{4,16},{6,18},{8,20},{10,22},{12,24},{14,26},{16,28}... | collective-permute-start | bytes 1032200 | tf_op jit(solution)/shard_map/ppermute | solution.py:25
  109.6 88.7 %collective-permute-start.10 = (bf16[1,42,4096]{2,1,0:T(8,128)(2,1)}, bf16[1,42,4096]{2,1,0:T(8,128)(2,1)S(1)}, u32[]{:S(2)}, u32[]{:S(2)}) collective-permute-start(bf16[1,42,4096]{2,1,0:T(8,128)(2,1)} %get-tuple-element.21), channel_id=1, source_target_pairs={{0,10},{2,12},{4,14},{6,16},{8,18},{10,20},{12,22},{14,24},{16,26}... | collective-permute-start | bytes 1032200 | tf_op jit(solution)/shard_map/ppermute | solution.py:25
  119.6 82.8 %collective-permute-start.11 = (bf16[1,42,4096]{2,1,0:T(8,128)(2,1)}, bf16[1,42,4096]{2,1,0:T(8,128)(2,1)S(1)}, u32[]{:S(2)}, u32[]{:S(2)}) collective-permute-start(bf16[1,42,4096]{2,1,0:T(8,128)(2,1)} %get-tuple-element.20), channel_id=1, source_target_pairs={{0,8},{2,10},{4,12},{6,14},{8,16},{10,18},{12,20},{14,22},{16,24},... | collective-permute-start | bytes 1032200 | tf_op jit(solution)/shard_map/ppermute | solution.py:25
  127.1 75.4 %collective-permute-start.12 = (bf16[1,42,4096]{2,1,0:T(8,128)(2,1)}, bf16[1,42,4096]{2,1,0:T(8,128)(2,1)S(1)}, u32[]{:S(2)}, u32[]{:S(2)}) collective-permute-start(bf16[1,42,4096]{2,1,0:T(8,128)(2,1)} %get-tuple-element.19), channel_id=1, source_target_pairs={{0,6},{2,8},{4,10},{6,12},{8,14},{10,16},{12,18},{14,20},{16,22},{... | collective-permute-start | bytes 1032200 | tf_op jit(solution)/shard_map/ppermute | solution.py:25
  155.3 51.6 %collective-permute-start.13 = (bf16[1,42,4096]{2,1,0:T(8,128)(2,1)S(1)}, bf16[1,42,4096]{2,1,0:T(8,128)(2,1)S(1)}, u32[]{:S(2)}, u32[]{:S(2)}) collective-permute-start(bf16[1,42,4096]{2,1,0:T(8,128)(2,1)S(1)} %copy-done.6), channel_id=1, source_target_pairs={{0,4},{2,6},{4,8},{6,10},{8,12},{10,14},{12,16},{14,18},{16,20},{1... | collective-permute-start | bytes 1032200 | tf_op jit(solution)/shard_map/ppermute | solution.py:25
  188.4 26.2 %collective-permute-start.14 = (bf16[1,42,4096]{2,1,0:T(8,128)(2,1)S(1)}, bf16[1,42,4096]{2,1,0:T(8,128)(2,1)S(1)}, u32[]{:S(2)}, u32[]{:S(2)}) collective-permute-start(bf16[1,42,4096]{2,1,0:T(8,128)(2,1)S(1)} %get-tuple-element.17), channel_id=1, source_target_pairs={{0,2},{2,4},{4,6},{6,8},{8,10},{10,12},{12,14},{14,16},{16,18},{18... | collective-permute-start | bytes 1032200 | tf_op jit(solution)/shard_map/ppermute | solution.py:25
  224.2 122.7 %reduce-scatter.2.cloned.1.call-start = ((), (), s32[]{:S(2)}) async-start(), calls=%async_computation.2 | async-start | bytes 18874368 | tf_op jit(solution)/shard_map/reduce_scatter | solution.py:107
  346.9 8.2 %copy-start.4 = (bf16[64,4096]{1,0:T(8,128)(2,1)S(1)}, bf16[64,4096]{1,0:T(8,128)(2,1)}, u32[]{:S(2)}) copy-start(bf16[64,4096]{1,0:T(8,128)(2,1)} %param.16) | copy-start | bytes 1572868
  346.9 9.1 %copy-start.5 = (bf16[1024,256]{1,0:T(8,128)(2,1)S(1)}, bf16[1024,256]{1,0:T(8,128)(2,1)}, u32[]{:S(2)}) copy-start(bf16[1024,256]{1,0:T(8,128)(2,1)} %param.20) | copy-start | bytes 1572868
  346.9 9.1 %copy-start.8 = (bf16[64,256]{1,0:T(8,128)(2,1)S(1)}, bf16[64,256]{1,0:T(8,128)(2,1)}, u32[]{:S(2)}) copy-start(bf16[64,256]{1,0:T(8,128)(2,1)} %param.18) | copy-start | bytes 98308
  346.9 147.1 %all-to-all-start = ((bf16[16,42,4096]{2,1,0:T(8,128)(2,1)}), bf16[16,42,4096]{2,1,0:T(8,128)(2,1)}, u32[]{:S(2)}, u32[]{:S(2)}) async-start(bf16[16,42,4096]{2,1,0:T(8,128)(2,1)} %bitcast.96), calls=%async_computation.1 | async-start | bytes 12582912 | tf_op jit(solution)/shard_map/all_to_all | solution.py:110
  500.2 19.0 %copy-start.1 = (bf16[1,384,4096]{2,1,0:T(8,128)(2,1)S(1)}, bf16[1,384,4096]{2,1,0:T(8,128)(2,1)}, u32[]{:S(2)}) copy-start(bf16[1,384,4096]{2,1,0:T(8,128)(2,1)} %param.26) | copy-start | bytes 9437188
  (4 other events, 25.9 us)
Sparse Core Ops, SparseCore 0:
  224.3 33.1 all-gather.2
  323.8 23.1 reduce-scatter.1
